TPU v7x, 32 devices: a whole 2x2x4 slice. The times are simulated.
32 devices in a mesh: seq: 4 (over x, core), tp: 8 (over z, y).
Axes of the slice: x: 2, y: 2, z: 4, core: 2. Of those that a mesh axis runs over, the one named last changes fastest.
Arguments:
- hidden_in: bfloat16 [2048, 3584], P('seq', 'tp'), may hold values from -6 to 6
- mamba_gain: float32 [3584], replicated, may hold values from 0.1 to 1.9
- w_xz: bfloat16 [2, 1536, 3584], P(None, 'tp'), may hold values from -0.09375 to 0.09375
- w_bc: bfloat16 [3584, 128], replicated, may hold values from -0.09375 to 0.09375
- w_dt: bfloat16 [24, 3584], P('tp'), may hold values from -0.09375 to 0.09375
- dt_bias: float32 [24], P('tp'), may hold values from -2 to 0
- decay_rate: float32 [24], P('tp'), may hold values from 0.00024414062 to 0.3
- conv_x: float32 [4, 1536], P(None, 'tp'), may hold values from -3 to 3
- conv_bc: float32 [4, 128], replicated, may hold values from -3 to 3
- skip_gain: float32 [24], P('tp'), may hold values from 0.5 to 1.5
- inner_gain: float32 [1536], P('tp'), may hold values from 0.1 to 1.9
- w_out: bfloat16 [1536, 3584], P('tp'), may hold values from -0.15625 to 0.15625
- attn_gain: float32 [3584], replicated, may hold values from 0.1 to 1.9
- w_qkv: bfloat16 [3, 1792, 3584], P(None, 'tp'), may hold values from -0.13363062 to 0.13363062
- w_o: bfloat16 [1792, 3584], P('tp'), may hold values from -0.125 to 0.125
- seg_ids: int32 [2048], P('seq'), may hold values from 0 to 3, as said below
- pad_mask: int32 [2048], P('seq'), may hold values from 0 to 1, as said below
- tenant_bounds: int32 [4, 2], replicated, may hold values from 0 to 2048, as said below
Outputs:
- hidden_out: bfloat16 [2048, 3584], P('seq', 'tp')
- kv_cache: bfloat16 [2, 1792, 2048], P(None, 'tp', 'seq')
- tenant_states: float32 [4, 24, 64, 64], P(None, 'tp')
Inputs may be any that keep to these rules, and one draw needn't show every extreme that they name: seg_ids never falls along the tokens; each tenant is one run of at least 128 tokens. `pad_mask`: each tenant's padding is its last tokens, at least one and at most a quarter of its run. `tenant_bounds`: row t holds where tenant t's run in seg_ids starts and one past where it ends; the runs follow one another and cover all 2048 tokens.
All inputs are finite; a program needn't handle non-finite values.
Results may differ from a plain program's by a relative error of at most 0.017.
Values may be sent and summed in bfloat16 or wider, within the bound.
No kernel may reach another device: no remote copies, remote signals or barrier semaphores. Data moves between devices by JAX's collectives and lax.ppermute only.
A program may use at most 128 MiB of HBM per device.

v0:
```python
import jax
import jax.numpy as jnp
from jax import lax
from jax.sharding import PartitionSpec as P

HEADS_DEV = 1
HIGHEST = lax.Precision.HIGHEST


def from_behind(value, axis, by):
    devices = lax.axis_size(axis)
    pairs = [(i, i + by) for i in range(devices) if 0 <= i + by < devices]
    return lax.ppermute(value, axis, pairs)


def rms_scale(rows):
    return lax.rsqrt(jnp.mean(rows * rows, axis=-1, keepdims=True) + 1e-05)


def times_rows(left, weights):
    return lax.dot_general(
        left, weights, (((1,), (1,)), ((), ())), preferred_element_type=jnp.float32
    )


def tenant_of(places, run_starts):
    return jnp.sum((places[:, None] >= run_starts[None, :]).astype(jnp.int32), axis=1) - 1


def row_terms(weights, activations):
    return lax.dot_general(
        weights, activations, (((0,), (1,)), ((), ())), preferred_element_type=jnp.float32
    )


def attend_block(
    carry,
    piece,
    start,
    query_heads,
    query_places,
    query_tenant,
    first_start,
    run_starts,
    head_count,
    score_scale,
):
    key_rows, value_rows, keep_rows = piece
    count = key_rows.shape[0]
    key_heads = key_rows.reshape(count, head_count, -1)
    value_heads = value_rows.reshape(count, head_count, -1)

    def update(state):
        running_max, running_total, running_sum = state
        key_places = jnp.arange(count, dtype=jnp.int32)
        key_tenant = tenant_of(key_places, run_starts)
        visible = (
            (key_tenant[None, :] == query_tenant[:, None])
            & (key_places[None, :] <= query_places[:, None])
            & (keep_rows[None, :] > 0)
        )
        scores = (
            jnp.einsum("qhd,khd->hqk", query_heads, key_heads, preferred_element_type=jnp.float32)
            * score_scale
        )
        scores = jnp.where(visible[None], scores, -1e30)
        fresh_max = jnp.maximum(running_max, jnp.max(scores, axis=-1))
        weights = jnp.exp(scores - fresh_max[..., None]) * visible[None].astype(jnp.float32)
        running_total = jnp.sum(weights, axis=-1)
        running_sum = jnp.einsum(
            "hqk,khd->hqd",
            weights.astype(jnp.bfloat16),
            value_heads,
            preferred_element_type=jnp.float32,
        )
        return (fresh_max, running_total, running_sum)

    wanted = (start <= query_places[-1]) & (start + count - 1 >= first_start)
    return lax.cond(wanted, update, lambda state: state, carry)


def on_device(
    hidden_in,
    mamba_gain,
    w_xz,
    w_bc,
    w_dt,
    dt_bias,
    decay_rate,
    conv_x,
    conv_bc,
    skip_gain,
    inner_gain,
    w_out,
    attn_gain,
    w_qkv,
    w_o,
    seg_ids,
    pad_mask,
    tenant_bounds,
):
    tok_rows = hidden_in.shape[0]
    width = mamba_gain.shape[0]
    tp_count = lax.axis_size("tp")
    seq_base = lax.axis_index("seq") * tok_rows
    places = seq_base + jnp.arange(tok_rows, dtype=jnp.int32)
    run_starts = tenant_bounds[:, 0]
    run_ends = tenant_bounds[:, 1]
    tenant_count = tenant_bounds.shape[0]
    full_in = lax.all_gather(hidden_in, "tp", axis=1, tiled=True)
    wide = full_in.astype(jnp.float32)
    normed = (wide * rms_scale(wide) * mamba_gain).astype(jnp.bfloat16)
    inner_dev = w_xz.shape[1]
    projected = times_rows(normed, w_xz.reshape(2 * inner_dev, width))
    bc_raw = jnp.dot(normed, w_bc, preferred_element_type=jnp.float32)
    live_rows = pad_mask.astype(jnp.float32)
    step_size = jax.nn.softplus(times_rows(normed, w_dt) + dt_bias) * live_rows[:, None]
    raw_input = jnp.concatenate([projected[:, :inner_dev], bc_raw], axis=1)
    conv_kernel = jnp.concatenate([conv_x, conv_bc], axis=1)
    tap_count = conv_kernel.shape[0]
    before = from_behind(raw_input[tok_rows - (tap_count - 1) :], "seq", 1)
    extended = jnp.concatenate([before, raw_input], axis=0)
    before_places = seq_base - (tap_count - 1) + jnp.arange(tap_count - 1, dtype=jnp.int32)
    ext_tenant = jnp.concatenate([tenant_of(before_places, run_starts), seg_ids])
    conv_sum = jnp.zeros_like(raw_input)
    for tap_row in range(tap_count):
        same_tenant = (ext_tenant[tap_row : tap_row + tok_rows] == seg_ids).astype(jnp.float32)
        conv_sum = (
            conv_sum
            + conv_kernel[tap_row] * extended[tap_row : tap_row + tok_rows] * same_tenant[:, None]
        )
    activated = jax.nn.silu(conv_sum)
    state_size = w_bc.shape[1] // 2
    heads_dev = decay_rate.shape[0]
    head_dim = inner_dev // heads_dev
    x_heads = activated[:, :inner_dev].reshape(tok_rows, heads_dev, head_dim)
    input_b = activated[:, inner_dev : inner_dev + state_size]
    output_c = activated[:, inner_dev + state_size :]
    begins = (ext_tenant[tap_count - 2 : tap_count - 2 + tok_rows] != seg_ids).astype(jnp.int32)
    run_label = jnp.cumsum(begins)
    log_total = jnp.cumsum(-step_size * decay_rate, axis=0).T
    row_number = jnp.arange(tok_rows, dtype=jnp.int32)
    lower_same = (row_number[None, :] <= row_number[:, None]) & (
        run_label[:, None] == run_label[None, :]
    )
    log_gap = log_total[:, :, None] - log_total[:, None, :]
    decay_pairs = jnp.where(lower_same[None], jnp.exp(jnp.minimum(log_gap, 0.0)), 0.0)
    c_dot_b = jnp.dot(output_c, input_b.T, precision=HIGHEST)
    mixing = decay_pairs * c_dot_b[None] * step_size.T[:, None, :]
    y_local = jnp.einsum("hij,jhp->ihp", mixing, x_heads, precision=HIGHEST)
    picked = jnp.concatenate(
        [
            jnp.clip(run_ends - 1 - seq_base, 0, tok_rows - 1),
            jnp.full((1,), tok_rows - 1, jnp.int32),
        ]
    )
    owned = ((run_ends - 1 >= seq_base) & (run_ends - 1 < seq_base + tok_rows)).astype(jnp.float32)
    picked_hot = row_number[None, :] == picked[:, None]
    log_picked = jnp.dot(picked_hot.astype(jnp.float32), log_total.T, precision=HIGHEST)
    run_picked = jnp.sum(jnp.where(picked_hot, run_label[None, :], 0), axis=1)
    reaching = (row_number[None, :] <= picked[:, None]) & (
        run_label[None, :] == run_picked[:, None]
    )
    toward = (
        jnp.where(
            reaching[:, None, :],
            jnp.exp(jnp.minimum(log_picked[:, :, None] - log_total[None], 0.0)),
            0.0,
        )
        * step_size.T[None]
    )
    local_states = jnp.einsum("khj,jhp,jn->khpn", toward, x_heads, input_b, precision=HIGHEST)
    carry_factor = jnp.exp(log_picked) * (run_picked == 0).astype(jnp.float32)[:, None]
    block_decay = carry_factor[-1]
    block_state = local_states[-1]
    incoming = jnp.zeros_like(block_state)
    for hop_count in range(lax.axis_size("seq") - 1):
        incoming = from_behind(
            (block_decay[:, None, None] * incoming + block_state).astype(jnp.bfloat16), "seq", 1
        ).astype(jnp.float32)
    entry_factor = jnp.exp(log_total.T) * (run_label == 0).astype(jnp.float32)[:, None]
    y_carry = (
        jnp.einsum("in,hpn->ihp", output_c, incoming, precision=HIGHEST) * entry_factor[:, :, None]
    )
    tenant_part = (carry_factor[:-1, :, None, None] * incoming[None] + local_states[:-1]) * owned[
        :, None, None, None
    ]
    tenant_states = lax.psum(tenant_part.astype(jnp.bfloat16), "seq").astype(jnp.float32)
    y_full = y_local + y_carry + skip_gain[None, :, None] * x_heads
    gated = y_full.reshape(tok_rows, inner_dev) * jax.nn.silu(projected[:, inner_dev:])
    square_sum = lax.psum(jnp.sum(gated * gated, axis=1), "tp")
    inner_scale = lax.rsqrt(square_sum / (inner_dev * tp_count) + 1e-05)
    scaled = (gated * inner_scale[:, None] * inner_gain).astype(jnp.bfloat16)
    my_rows = lax.psum_scatter(
        row_terms(w_out, scaled).astype(jnp.bfloat16), "tp", scatter_dimension=0, tiled=True
    ).astype(jnp.float32)
    mixed_part = (hidden_in.astype(jnp.float32) + my_rows.T).astype(jnp.bfloat16)
    after_mix = lax.all_gather(mixed_part, "tp", axis=1, tiled=True)
    wide_mix = after_mix.astype(jnp.float32)
    normed_attn = (wide_mix * rms_scale(wide_mix) * attn_gain).astype(jnp.bfloat16)
    att_dev = w_qkv.shape[1]
    qkv_rows = times_rows(normed_attn, w_qkv.reshape(3 * att_dev, width)).astype(jnp.bfloat16)
    key_rows = qkv_rows[:, att_dev : 2 * att_dev]
    value_rows = qkv_rows[:, 2 * att_dev :]
    kv_cache = jnp.stack([key_rows.T, value_rows.T])
    head_count = HEADS_DEV
    head_size = att_dev // head_count
    query_heads = qkv_rows[:, :att_dev].reshape(tok_rows, head_count, head_size)
    keep_rows = pad_mask.astype(jnp.bfloat16)
    first_start = jnp.sum(
        jnp.where(jnp.arange(tenant_count, dtype=jnp.int32) == seg_ids[0], run_starts, 0)
    )
    score_scale = head_size ** (-0.5)
    initial = (
        jnp.full((head_count, tok_rows), -1e30, jnp.float32),
        jnp.zeros((head_count, tok_rows), jnp.float32),
        jnp.zeros((head_count, tok_rows, head_size), jnp.float32),
    )
    running_max, running_total, running_sum = attend_block(
        initial,
        (
            lax.all_gather(key_rows, "seq", axis=0, tiled=True),
            lax.all_gather(value_rows, "seq", axis=0, tiled=True),
            lax.all_gather(keep_rows, "seq", axis=0, tiled=True),
        ),
        jnp.int32(0),
        query_heads,
        places,
        seg_ids,
        first_start,
        run_starts,
        head_count,
        score_scale,
    )
    context = (running_sum / running_total[..., None]).astype(jnp.bfloat16)
    context_rows = context.transpose(1, 0, 2).reshape(tok_rows, att_dev)
    attn_part = lax.psum_scatter(
        row_terms(w_o, context_rows).astype(jnp.bfloat16), "tp", scatter_dimension=0, tiled=True
    ).astype(jnp.float32)
    hidden_out = (mixed_part.astype(jnp.float32) + attn_part.T).astype(jnp.bfloat16)
    return (hidden_out, kv_cache, tenant_states)


def solution(mesh):
    return jax.shard_map(
        on_device,
        mesh=mesh,
        in_specs=(
            P("seq", "tp"),
            P(),
            P(None, "tp", None),
            P(),
            P("tp", None),
            P("tp"),
            P("tp"),
            P(None, "tp"),
            P(),
            P("tp"),
            P("tp"),
            P("tp", None),
            P(),
            P(None, "tp", None),
            P("tp", None),
            P("seq"),
            P("seq"),
            P(),
        ),
        out_specs=(P("seq", "tp"), P(None, "tp", "seq"), P(None, "tp", None, None)),
        check_vma=False,
    )
```

profile of v0, /device:TPU:0, one launch (start us, length us, event | category | flops | bytes accessed | tf_op | source)
XLA Modules:
  0.0 445.4 jit_solution(3268128073207426532)
XLA Ops:
  13.4 66.4 %all-gather.4.cloned.1.call-done = bf16[512,3584]{0,1:T(8,128)(2,1)} async-done(((bf16[512,448]{0,1:T(8,128)(2,1)}), bf16[512,3584]{0,1:T(8,128)(2,1)}) %all-gather.4.cloned.1.call-update) | async-done | bytes 3670032 | tf_op jit(solution)/shard_map/all_gather | solution.py:110
  79.8 2.9 fusion.16
  82.7 3.3 negate_multiply_fusion
  87.8 3.9 fusion.99
  98.4 5.3 %collective-permute-start.1 = (bf16[3,64,64]{2,1,0:T(8,128)(2,1)S(1)}, bf16[3,64,64]{2,1,0:T(8,128)(2,1)S(1)}, u32[]{:S(2)}, u32[]{:S(2)}) collective-permute-start(bf16[3,64,64]{2,1,0:T(8,128)(2,1)S(1)} %add_convert_fusion.2), channel_id=1, source_target_pairs={{0,8},{8,16},{16,24},{1,9},{9,17},{17,25},{2,10},{10,18},{18,26},{... | collective-permute-start | bytes 73736 | tf_op jit(solution)/shard_map/ppermute | solution.py:13
  104.7 4.7 %collective-permute-start.2 = (bf16[3,64,64]{2,1,0:T(8,128)(2,1)S(1)}, bf16[3,64,64]{2,1,0:T(8,128)(2,1)S(1)}, u32[]{:S(2)}, u32[]{:S(2)}) collective-permute-start(bf16[3,64,64]{2,1,0:T(8,128)(2,1)S(1)} %add_convert_fusion.1), channel_id=1, source_target_pairs={{0,8},{8,16},{16,24},{1,9},{9,17},{17,25},{2,10},{10,18},{18,26},{... | collective-permute-start | bytes 73736 | tf_op jit(solution)/shard_map/ppermute | solution.py:13
  110.5 4.5 %collective-permute-start.3 = (bf16[3,64,64]{2,1,0:T(8,128)(2,1)S(1)}, bf16[3,64,64]{2,1,0:T(8,128)(2,1)S(1)}, u32[]{:S(2)}, u32[]{:S(2)}) collective-permute-start(bf16[3,64,64]{2,1,0:T(8,128)(2,1)S(1)} %add_convert_fusion), channel_id=1, source_target_pairs={{0,8},{8,16},{16,24},{1,9},{9,17},{17,25},{2,10},{10,18},{18,26},{... | collective-permute-start | bytes 73736 | tf_op jit(solution)/shard_map/ppermute | solution.py:13
  115.1 3.9 fusion.49
  119.5 18.9 %psum.14 = f32[512]{0:T(512)S(1)} all-reduce(f32[512]{0:T(512)S(1)} %get-tuple-element.77), channel_id=1, replica_groups=mesh['seq'=4,'tp'=8] {'tp'}, use_global_device_ids=true, to_apply=%region_8.9 | all-reduce | flops 512 | bytes 4096 | tf_op jit(solution)/shard_map/psum | solution.py:191
  138.4 4.4 fusion.22
  142.8 6.0 %copy.50 = bf16[3584,512]{1,0:T(8,128)(2,1)} copy(bf16[3584,512]{0,1:T(8,128)(2,1)} %fusion.22) | data formatting | bytes 7340032
  149.9 78.3 %reduce-scatter.7.cloned.1.call-done = bf16[448,512]{1,0:T(8,128)(2,1)} async-done(((bf16[3584,512]{1,0:T(8,128)(2,1)}), bf16[448,512]{1,0:T(8,128)(2,1)}) %reduce-scatter.7.cloned.1.call-update) | async-done | bytes 458768
  236.1 5.2 %all-gather = bf16[4,1,512]{2,1,0:T(2,128)(2,1)S(1)} all-gather(bf16[1,1,512]{2,1,0:T(2,128)(2,1)S(1)} %reshape.310), channel_id=1, replica_groups=mesh['seq'=4,'tp'=8] {'seq'}, dimensions={0}, use_global_device_ids=true | all-gather | bytes 5120 | tf_op jit(solution)/shard_map/all_gather | solution.py:224
  243.2 55.9 %all-gather.6.cloned.1.call-done = bf16[512,3584]{0,1:T(8,128)(2,1)} async-done(((bf16[512,448]{0,1:T(8,128)(2,1)}), bf16[512,3584]{0,1:T(8,128)(2,1)}) %all-gather.6.cloned.1.call-update) | async-done | bytes 3670032 | tf_op jit(solution)/shard_map/all_gather | solution.py:198
  299.2 2.9 fusion.19
  302.1 7.1 %fusion.43 = bf16[512,672]{0,1:T(8,128)(2,1)} fusion(bf16[672,3584]{1,0:T(8,128)(2,1)} %bitcast.115, bf16[512,3584]{0,1:T(8,128)(2,1)} %all-gather.6.cloned.1.call-done, f32[3584]{0:T(1024)S(1)} %copy-done.12, f32[512]{0:T(512)S(1)} %add_rsqrt_fusion), kind=kOutput, calls=%fused_computation.52 | convolution fusion | flops 2473934848 | bytes 9191424 | tf_op jit(solution)/shard_map/dot_general | solution.py:21
  311.0 9.7 %all_gather.19 = bf16[2048,224]{0,1:T(8,128)(2,1)} all-gather(bf16[512,224]{0,1:T(8,128)(2,1)S(1)} %get-tuple-element.85), channel_id=1, replica_groups=mesh['seq'=4,'tp'=8] {'seq'}, dimensions={0}, use_global_device_ids=true | all-gather | bytes 1146880 | tf_op jit(solution)/shard_map/all_gather | solution.py:223
  320.7 11.1 %all_gather.18 = bf16[2048,224]{0,1:T(8,128)(2,1)} all-gather(bf16[512,224]{0,1:T(8,128)(2,1)S(1)} %get-tuple-element.86), channel_id=1, replica_groups=mesh['seq'=4,'tp'=8] {'seq'}, dimensions={0}, use_global_device_ids=true | all-gather | bytes 1146880 | tf_op jit(solution)/shard_map/all_gather | solution.py:222
  331.8 10.9 %conditional.1 = (f32[1,512]{1,0:T(1,128)S(1)}, f32[1,512,224]{1,2,0:T(8,128)}) conditional(s32[]{:T(128)} %convert_element_type.146, () %tuple.16, (s32[4,1]{0,1:T(1,128)S(1)}, s32[512]{0:T(512)S(1)}, s32[512]{0:T(512)S(1)}, bf16[4,1,512]{2,1,0:T(2,128)(2,1)S(1)}, bf16[512,672]{0,1:T(8,128)(2,1)}, /*index=5*/bf16[2048,224]{0,1:T(8,128)(2,1)}, ...), branch_computations={%region_12.13_spmd, %region_13.17_spmd} | conditional | flops 965764608 | bytes 20287550 | solution.py:79
  334.2 3.1 fusion.2
  337.4 3.1 fusion.7
  342.7 4.6 %fusion.23 = bf16[3584,512]{0,1:T(8,128)(2,1)} fusion(bf16[224,3584]{1,0:T(8,128)(2,1)} %param.34, f32[1,512,224]{1,2,0:T(8,128)} %get-tuple-element.30, f32[512]{0:T(512)S(1)} %bitcast.107), kind=kOutput, calls=%fused_computation.33 | convolution fusion | flops 824147968 | bytes 5736448 | tf_op jit(solution)/shard_map/dot_general | solution.py:31
  347.3 5.9 %copy.52 = bf16[3584,512]{1,0:T(8,128)(2,1)} copy(bf16[3584,512]{0,1:T(8,128)(2,1)} %fusion.23) | data formatting | bytes 7340032
  356.7 76.2 %reduce-scatter.9.cloned.1.call-done = bf16[448,512]{1,0:T(8,128)(2,1)} async-done(((bf16[3584,512]{1,0:T(8,128)(2,1)}), bf16[448,512]{1,0:T(8,128)(2,1)}) %reduce-scatter.9.cloned.1.call-update) | async-done | bytes 458768
  (117 shorter events, 42.8 us)
Async XLA Ops:
  7.2 80.6 %copy-start = (bf16[2,192,3584]{2,1,0:T(8,128)(2,1)S(1)}, bf16[2,192,3584]{2,1,0:T(8,128)(2,1)}, u32[]{:S(2)}) copy-start(bf16[2,192,3584]{2,1,0:T(8,128)(2,1)} %param.22) | copy-start | bytes 8257540
  7.2 75.5 %copy-start.11 = (f32[3584]{0:T(1024)S(1)}, f32[3584]{0:T(1024)}, u32[]{:S(2)}) copy-start(f32[3584]{0:T(1024)} %param.21) | copy-start | bytes 43012
  7.2 75.5 %copy-start.13 = (f32[3]{0:T(128)S(1)}, f32[3]{0:T(128)}, u32[]{:S(2)}) copy-start(f32[3]{0:T(128)} %param.26) | copy-start | bytes 40
  7.2 75.5 %copy-start.14 = (f32[3]{0:T(128)S(1)}, f32[3]{0:T(128)}, u32[]{:S(2)}) copy-start(f32[3]{0:T(128)} %param.25) | copy-start | bytes 40
  7.2 75.5 %copy-start.10 = (bf16[3,3584]{1,0:T(4,128)(2,1)S(1)}, bf16[3,3584]{1,0:T(4,128)(2,1)}, u32[]{:S(2)}) copy-start(bf16[3,3584]{1,0:T(4,128)(2,1)} %param.24) | copy-start | bytes 64516
  7.2 72.6 %all-gather.4.cloned.1.call-start = ((), (), s32[]{:S(2)}) async-start(), calls=%async_computation.2 | async-start | bytes 4128768 | tf_op jit(solution)/shard_map/all_gather | solution.py:110
  8.0 220.2 %reduce-scatter.7.cloned.1.call-start = ((), (), s32[]{:S(2)}) async-start(), calls=%async_computation.5 | async-start | bytes 4128768
  87.8 3.9 copy-start.1
  87.8 3.9 copy-start.9
  93.3 2.3 collective-permute-start
  98.3 12.1 %copy-start.2 = (f32[5,3,64,64]{3,2,0,1:T(8,128)}, f32[5,3,64,64]{3,2,0,1:T(8,128)S(1)}, u32[]{:S(2)}) copy-start(f32[5,3,64,64]{3,2,0,1:T(8,128)S(1)} %fusion.46) | copy-start | bytes 737284
  98.3 20.7 %copy-start.8 = (f32[3]{0:T(128)S(1)}, f32[3]{0:T(128)}, u32[]{:S(2)}) copy-start(f32[3]{0:T(128)} %param.29) | copy-start | bytes 40
  98.4 6.2 %collective-permute-start.1 = (bf16[3,64,64]{2,1,0:T(8,128)(2,1)S(1)}, bf16[3,64,64]{2,1,0:T(8,128)(2,1)S(1)}, u32[]{:S(2)}, u32[]{:S(2)}) collective-permute-start(bf16[3,64,64]{2,1,0:T(8,128)(2,1)S(1)} %add_convert_fusion.2), channel_id=1, source_target_pairs={{0,8},{8,16},{16,24},{1,9},{9,17},{17,25},{2,10},{10,18},{18,26},{... | collective-permute-start | bytes 73736 | tf_op jit(solution)/shard_map/ppermute | solution.py:13
  104.7 5.7 %collective-permute-start.2 = (bf16[3,64,64]{2,1,0:T(8,128)(2,1)S(1)}, bf16[3,64,64]{2,1,0:T(8,128)(2,1)S(1)}, u32[]{:S(2)}, u32[]{:S(2)}) collective-permute-start(bf16[3,64,64]{2,1,0:T(8,128)(2,1)S(1)} %add_convert_fusion.1), channel_id=1, source_target_pairs={{0,8},{8,16},{16,24},{1,9},{9,17},{17,25},{2,10},{10,18},{18,26},{... | collective-permute-start | bytes 73736 | tf_op jit(solution)/shard_map/ppermute | solution.py:13
  110.5 27.8 %copy-start.6 = (f32[192]{0:T(256)S(1)}, f32[192]{0:T(256)}, u32[]{:S(2)}) copy-start(f32[192]{0:T(256)} %param.30) | copy-start | bytes 2308
  110.5 8.4 %collective-permute-start.3 = (bf16[3,64,64]{2,1,0:T(8,128)(2,1)S(1)}, bf16[3,64,64]{2,1,0:T(8,128)(2,1)S(1)}, u32[]{:S(2)}, u32[]{:S(2)}) collective-permute-start(bf16[3,64,64]{2,1,0:T(8,128)(2,1)S(1)} %add_convert_fusion), channel_id=1, source_target_pairs={{0,8},{8,16},{16,24},{1,9},{9,17},{17,25},{2,10},{10,18},{18,26},{... | collective-permute-start | bytes 73736 | tf_op jit(solution)/shard_map/ppermute | solution.py:13
  142.8 6.1 %copy-start.3 = (bf16[512,448]{0,1:T(8,128)(2,1)S(1)}, bf16[512,448]{0,1:T(8,128)(2,1)}, u32[]{:S(2)}) copy-start(bf16[512,448]{0,1:T(8,128)(2,1)} %param.20) | copy-start | bytes 1376260
  148.7 83.8 %copy-start.5 = (s32[512]{0:T(512)S(1)}, s32[512]{0:T(512)}, u32[]{:S(2)}) copy-start(s32[512]{0:T(512)} %param.35) | copy-start | bytes 6148
  148.7 84.9 %copy-start.7 = (s32[4,2]{0,1:T(2,128)S(1)}, s32[4,2]{0,1:T(2,128)}, u32[]{:S(2)}) copy-start(s32[4,2]{0,1:T(2,128)} %param.37) | copy-start | bytes 100
  148.8 150.4 %all-gather.6.cloned.1.call-start = ((), (), s32[]{:S(2)}) async-start(), calls=%async_computation.3 | async-start | bytes 4128768 | tf_op jit(solution)/shard_map/all_gather | solution.py:198
  149.9 152.2 %copy-start.12 = (f32[3584]{0:T(1024)S(1)}, f32[3584]{0:T(1024)}, u32[]{:S(2)}) copy-start(f32[3584]{0:T(1024)} %param.32) | copy-start | bytes 43012
  232.5 120.8 %all-reduce.2.cloned.1.call-start = ((), (), s32[]{:S(2)}) async-start(), calls=%async_computation.4 | async-start | bytes 393216 | tf_op jit(solution)/shard_map/psum | solution.py:188
  243.2 189.7 %reduce-scatter.9.cloned.1.call-start = ((), (), s32[]{:S(2)}) async-start(), calls=%async_computation.6 | async-start | bytes 4128768
  334.2 3.1 copy-start.4
Sparse Core Ops, SparseCore 0:
  10.2 69.5 all-gather.3
  148.9 79.2 reduce-scatter.6
  232.6 66.5 all-gather.5
  301.9 30.5 all-reduce.1
  353.4 79.4 reduce-scatter.8
where the time goes:
time: 447 us; the launch traced here: 445 us
  waiting for transfers between devices  279 us (62%)
  blocking collectives  44.9 us (10%)
  matrix products  38 us (9%)
  local copies, waits for them, and re-layouts  27.5 us (6%)
  other arithmetic  24.2 us (5%)
  starting transfers between devices  16 us (4%)
  between operations  15.4 us (3%)
    unnamed x7, waiting for transfers between devices  155 us
    all_gather x1, waiting for transfers between devices, on_device(): full_in = lax.all_gather(hidden_in, 'tp', axis=1, tiled=True)  66.4 us
    all_gather x1, waiting for transfers between devices, on_device(): after_mix = lax.all_gather(mixed_part, 'tp', axis=1, tiled=True)  55.9 us
    unnamed x37, local copies, waits for them, and re-layouts  20.7 us
    psum x1, blocking collectives, on_device(): square_sum = lax.psum(jnp.sum(gated * gated, axis=1), 'tp')  18.9 us
    ppermute x4, starting transfers between devices, from_behind(): return lax.ppermute(value, axis, pairs)  15.8 us
    dot_general x3, matrix products, times_rows(): lax.dot_general(left, weights, (((1,), (1,)), ((), ())), preferred_elemen...  14.3 us
    all_gather x1, blocking collectives, on_device(): lax.all_gather(key_rows, 'seq', axis=0, tiled=True)  11.1 us
  transfers between devices with their start and end apart: 9, of which 6 were waited for; matrix products, arithmetic and copies ran while one was open for 12% of the time, Pallas kernels for 0%

commit v1 on v0

--- a/solution.py
+++ b/solution.py
@@ -5,6 +5,19 @@
 
 HEADS_DEV = 1
 HIGHEST = lax.Precision.HIGHEST
+
+
+def ring_gather(x, axis, dim):
+    ways = lax.axis_size(axis)
+    up = [(d, (d + 1) % ways) for d in range(ways)]
+    down = [(d, (d - 1) % ways) for d in range(ways)]
+    earlier, later = ([x], [x])
+    for _ in range(ways // 2):
+        earlier.append(lax.ppermute(earlier[-1], axis, up))
+    for _ in range((ways - 1) // 2):
+        later.append(lax.ppermute(later[-1], axis, down))
+    line = jnp.concatenate([*earlier[::-1], *later[1:]], axis=dim)
+    return jnp.roll(line, (lax.axis_index(axis) - ways // 2) * x.shape[dim], axis=dim)
 
 
 def from_behind(value, axis, by):
@@ -220,7 +233,7 @@
         initial,
         (
             lax.all_gather(key_rows, "seq", axis=0, tiled=True),
-            lax.all_gather(value_rows, "seq", axis=0, tiled=True),
+            ring_gather(value_rows, "seq", 0),
             lax.all_gather(keep_rows, "seq", axis=0, tiled=True),
         ),
         jnp.int32(0),

time: 447 us -> 466 us (1.043)
  local copies, waits for them, and re-layouts: 27.5 us -> 44.8 us
  blocking collectives: 44.9 us -> 34.6 us
  waiting for transfers between devices: 279 us -> 287 us
    unnamed x37 -> x61, local copies, waits for them, and re-layouts: 20.7 us -> 31.2 us
    all_gather x1 -> x0, blocking collectives: 9.73 us -> none  [on_device(): lax.all_gather(value_rows, 'seq', axis=0, tiled=True)]
    all_gather x1, waiting for transfers between devices: 55.9 us -> 64.2 us  [on_device(): after_mix = lax.all_gather(mixed_part, 'tp', axis=1, tiled=True)]
  transfers between devices with their start and end apart: 9 -> 12, of which waited for: 6 -> 7; matrix products, arithmetic and copies ran while one was open for 12% -> 14% of each run, Pallas kernels for 0% -> 0%
where the time goes in v1:
time: 466 us; the launch traced here: 465 us
  waiting for transfers between devices  287 us (62%)
  local copies, waits for them, and re-layouts  44.8 us (10%)
  matrix products  38 us (8%)
  blocking collectives  34.6 us (7%)
  other arithmetic  26.8 us (6%)
  starting transfers between devices  17.9 us (4%)
  between operations  15.5 us (3%)
    unnamed x7, waiting for transfers between devices  154 us
    all_gather x1, waiting for transfers between devices, on_device(): full_in = lax.all_gather(hidden_in, 'tp', axis=1, tiled=True)  65.3 us
    all_gather x1, waiting for transfers between devices, on_device(): after_mix = lax.all_gather(mixed_part, 'tp', axis=1, tiled=True)  64.2 us
    unnamed x61, local copies, waits for them, and re-layouts  31.2 us
    psum x1, blocking collectives, on_device(): square_sum = lax.psum(jnp.sum(gated * gated, axis=1), 'tp')  18.9 us
    ppermute x4, starting transfers between devices, from_behind(): return lax.ppermute(value, axis, pairs)  15.8 us
    dot_general x3, matrix products, times_rows(): lax.dot_general(left, weights, (((1,), (1,)), ((), ())), preferred_elemen...  9.95 us
  transfers between devices with their start and end apart: 12, of which 7 were waited for; matrix products, arithmetic and copies ran while one was open for 14% of the time, Pallas kernels for 0%

profile of v1, /device:TPU:0, one launch (start us, length us, event | category | flops | bytes accessed | tf_op | source)
XLA Modules:
  0.0 465.0 jit_solution(6031305998338953485)
XLA Ops:
  14.4 65.3 %all-gather.4.cloned.1.call-done = bf16[512,3584]{0,1:T(8,128)(2,1)} async-done(((bf16[512,448]{0,1:T(8,128)(2,1)}), bf16[512,3584]{0,1:T(8,128)(2,1)}) %all-gather.4.cloned.1.call-update) | async-done | bytes 3670032 | tf_op jit(solution)/shard_map/all_gather | solution.py:123
  79.8 3.0 fusion.18
  85.5 3.9 fusion.101
  96.1 5.3 %collective-permute-start.1 = (bf16[3,64,64]{2,1,0:T(8,128)(2,1)S(1)}, bf16[3,64,64]{2,1,0:T(8,128)(2,1)S(1)}, u32[]{:S(2)}, u32[]{:S(2)}) collective-permute-start(bf16[3,64,64]{2,1,0:T(8,128)(2,1)S(1)} %add_convert_fusion.2), channel_id=1, source_target_pairs={{0,8},{8,16},{16,24},{1,9},{9,17},{17,25},{2,10},{10,18},{18,26},{... | collective-permute-start | bytes 73736 | tf_op jit(solution)/shard_map/ppermute | solution.py:26
  102.4 4.7 %collective-permute-start.2 = (bf16[3,64,64]{2,1,0:T(8,128)(2,1)S(1)}, bf16[3,64,64]{2,1,0:T(8,128)(2,1)S(1)}, u32[]{:S(2)}, u32[]{:S(2)}) collective-permute-start(bf16[3,64,64]{2,1,0:T(8,128)(2,1)S(1)} %add_convert_fusion.1), channel_id=1, source_target_pairs={{0,8},{8,16},{16,24},{1,9},{9,17},{17,25},{2,10},{10,18},{18,26},{... | collective-permute-start | bytes 73736 | tf_op jit(solution)/shard_map/ppermute | solution.py:26
  108.2 4.5 collective-permute-start.3
  112.7 3.9 fusion.51
  117.2 18.9 %psum.14 = f32[512]{0:T(512)S(1)} all-reduce(f32[512]{0:T(512)S(1)} %get-tuple-element.210), channel_id=1, replica_groups=mesh['seq'=4,'tp'=8] {'tp'}, use_global_device_ids=true, to_apply=%region_8.9 | all-reduce | flops 512 | bytes 4096 | tf_op jit(solution)/shard_map/psum | solution.py:204
  136.0 4.4 fusion.24
  140.5 5.9 %copy.49 = bf16[3584,512]{1,0:T(8,128)(2,1)} copy(bf16[3584,512]{0,1:T(8,128)(2,1)} %fusion.24) | data formatting | bytes 7340032
  148.4 77.4 %reduce-scatter.7.cloned.1.call-done = bf16[448,512]{1,0:T(8,128)(2,1)} async-done(((bf16[3584,512]{1,0:T(8,128)(2,1)}), bf16[448,512]{1,0:T(8,128)(2,1)}) %reduce-scatter.7.cloned.1.call-update) | async-done | bytes 458768
  232.6 64.2 %all-gather.6.cloned.1.call-done = bf16[512,3584]{0,1:T(8,128)(2,1)} async-done(((bf16[512,448]{0,1:T(8,128)(2,1)}), bf16[512,3584]{0,1:T(8,128)(2,1)}) %all-gather.6.cloned.1.call-update) | async-done | bytes 3670032 | tf_op jit(solution)/shard_map/all_gather | solution.py:211
  296.8 3.0 fusion.21
  299.9 5.1 %fusion.45 = bf16[512,672]{0,1:T(8,128)(2,1)S(1)} fusion(bf16[672,3584]{1,0:T(8,128)(2,1)} %bitcast.114, bf16[512,3584]{0,1:T(8,128)(2,1)S(1)} %copy-done.5, f32[3584]{0:T(1024)S(1)} %copy-done.21, f32[512]{0:T(512)S(1)} %add_rsqrt_fusion), kind=kOutput, calls=%fused_computation.54 | convolution fusion | flops 2473934848 | bytes 9191424 | tf_op jit(solution)/shard_map/dot_general | solution.py:34
  311.0 6.5 %all-gather = bf16[4,1,512]{2,1,0:T(2,128)(2,1)} all-gather(bf16[1,1,512]{2,1,0:T(2,128)(2,1)} %reshape.328), channel_id=1, replica_groups=mesh['seq'=4,'tp'=8] {'seq'}, dimensions={0}, use_global_device_ids=true | all-gather | bytes 5120 | tf_op jit(solution)/shard_map/all_gather | solution.py:237
  333.0 9.3 %all_gather.15 = bf16[2048,224]{0,1:T(8,128)(2,1)} all-gather(bf16[512,224]{0,1:T(8,128)(2,1)S(1)} %get-tuple-element.219), channel_id=1, replica_groups=mesh['seq'=4,'tp'=8] {'seq'}, dimensions={0}, use_global_device_ids=true | all-gather | bytes 1146880 | tf_op jit(solution)/shard_map/all_gather | solution.py:235
  343.1 19.5 %conditional.1 = (f32[1,512]{1,0:T(1,128)S(1)}, f32[1,512,224]{1,2,0:T(8,128)}) conditional(s32[]{:T(128)} %convert_element_type.152, () %tuple.27, (s32[4,1]{0,1:T(1,128)S(1)}, s32[512]{0:T(512)S(1)}, s32[512]{0:T(512)S(1)}, bf16[4,1,512]{2,1,0:T(2,128)(2,1)S(1)}, bf16[512,672]{0,1:T(8,128)(2,1)}, /*index=5*/bf16[2048,224]{0,1:T(8,128)(2,1)}, ...), branch_computations={%region_12.13_spmd, %region_13.17_spmd} | conditional | flops 965764608 | bytes 37195992 | solution.py:92
  345.7 4.8 %fusion.2 = (f32[512]{0:T(512)S(1)}, f32[512,2048]{1,0:T(8,128)}) fusion(pred[2048]{0:T(1024)(128)(4,1)S(1)} %broadcast_compare_fusion, s32[512]{0:T(512)S(1)} %get-tuple-element.123, s32[512]{0:T(512)S(1)} %get-tuple-element.122, s32[2048]{0:T(1024)S(1)} %broadcast_add_fusion, bf16[2048,224]{0,1:T(8,128)(2,1)} %get-tuple-element.193, bf16[512,672]{1,0:T(8,128)(2,1)} %copy.42), kind=kOutput, calls=%fused_computation.5 | convolution fusion | flops 477101568 | bytes 5390336 | tf_op jit(solution)/shard_map/cond/branch_1_fun/qhd,khd->hqk/dot_general | solution.py:76
  350.6 4.0 copy.44
  354.5 5.7 %fusion.7 = f32[1,512,224]{1,2,0:T(8,128)} fusion(f32[512,2048]{1,0:T(8,128)} %get-tuple-element.215, f32[512]{0:T(512)S(1)} %broadcast_maximum_fusion, bf16[4096,224]{1,0:T(8,128)(2,1)} %copy.44, s32[]{:T(128)S(6)} %select_n.44, s32[512]{0:T(512)S(1)} %get-tuple-element.123, s32[2048]{0:T(1024)S(1)} %broadcast_add_fusion, s32[512]{0:T(512)S(1)} %get-tuple-element.122, ...), kind=kOutput, calls=%fused_computation.9 | convolution fusion | flops 479199232 | bytes 5718020 | tf_op jit(solution)/shard_map/cond/branch_1_fun/hqk,khd->hqd/dot_general | solution.py:83
  360.3 2.3 fusion.4
  362.5 4.6 fusion.25
  367.1 5.9 %copy.51 = bf16[3584,512]{1,0:T(8,128)(2,1)} copy(bf16[3584,512]{0,1:T(8,128)(2,1)} %fusion.25) | data formatting | bytes 7340032
  376.5 75.9 %reduce-scatter.9.cloned.1.call-done = bf16[448,512]{1,0:T(8,128)(2,1)} async-done(((bf16[3584,512]{1,0:T(8,128)(2,1)}), bf16[448,512]{1,0:T(8,128)(2,1)}) %reduce-scatter.9.cloned.1.call-update) | async-done | bytes 458768
  (149 shorter events, 60.7 us)
Async XLA Ops:
  7.2 78.3 %copy-start = (bf16[2,192,3584]{2,1,0:T(8,128)(2,1)S(1)}, bf16[2,192,3584]{2,1,0:T(8,128)(2,1)}, u32[]{:S(2)}) copy-start(bf16[2,192,3584]{2,1,0:T(8,128)(2,1)} %param.22) | copy-start | bytes 8257540
  7.2 75.7 %copy-start.20 = (f32[3584]{0:T(1024)S(1)}, f32[3584]{0:T(1024)}, u32[]{:S(2)}) copy-start(f32[3584]{0:T(1024)} %param.21) | copy-start | bytes 43012
  7.2 75.6 %copy-start.19 = (bf16[3,3584]{1,0:T(4,128)(2,1)S(1)}, bf16[3,3584]{1,0:T(4,128)(2,1)}, u32[]{:S(2)}) copy-start(bf16[3,3584]{1,0:T(4,128)(2,1)} %param.24) | copy-start | bytes 64516
  7.2 75.6 %copy-start.23 = (f32[3]{0:T(128)S(1)}, f32[3]{0:T(128)}, u32[]{:S(2)}) copy-start(f32[3]{0:T(128)} %param.25) | copy-start | bytes 40
  7.2 75.6 %copy-start.22 = (f32[3]{0:T(128)S(1)}, f32[3]{0:T(128)}, u32[]{:S(2)}) copy-start(f32[3]{0:T(128)} %param.26) | copy-start | bytes 40
  7.2 72.6 %all-gather.4.cloned.1.call-start = ((), (), s32[]{:S(2)}) async-start(), calls=%async_computation.2 | async-start | bytes 4128768 | tf_op jit(solution)/shard_map/all_gather | solution.py:123
  8.0 217.8 %reduce-scatter.7.cloned.1.call-start = ((), (), s32[]{:S(2)}) async-start(), calls=%async_computation.5 | async-start | bytes 4128768
  91.0 2.3 collective-permute-start
  96.1 6.2 %collective-permute-start.1 = (bf16[3,64,64]{2,1,0:T(8,128)(2,1)S(1)}, bf16[3,64,64]{2,1,0:T(8,128)(2,1)S(1)}, u32[]{:S(2)}, u32[]{:S(2)}) collective-permute-start(bf16[3,64,64]{2,1,0:T(8,128)(2,1)S(1)} %add_convert_fusion.2), channel_id=1, source_target_pairs={{0,8},{8,16},{16,24},{1,9},{9,17},{17,25},{2,10},{10,18},{18,26},{... | collective-permute-start | bytes 73736 | tf_op jit(solution)/shard_map/ppermute | solution.py:26
  102.4 5.7 %collective-permute-start.2 = (bf16[3,64,64]{2,1,0:T(8,128)(2,1)S(1)}, bf16[3,64,64]{2,1,0:T(8,128)(2,1)S(1)}, u32[]{:S(2)}, u32[]{:S(2)}) collective-permute-start(bf16[3,64,64]{2,1,0:T(8,128)(2,1)S(1)} %add_convert_fusion.1), channel_id=1, source_target_pairs={{0,8},{8,16},{16,24},{1,9},{9,17},{17,25},{2,10},{10,18},{18,26},{... | collective-permute-start | bytes 73736 | tf_op jit(solution)/shard_map/ppermute | solution.py:26
  108.2 27.8 %copy-start.14 = (f32[192]{0:T(256)S(1)}, f32[192]{0:T(256)}, u32[]{:S(2)}) copy-start(f32[192]{0:T(256)} %param.30) | copy-start | bytes 2308
  108.2 8.4 %collective-permute-start.3 = (bf16[3,64,64]{2,1,0:T(8,128)(2,1)S(1)}, bf16[3,64,64]{2,1,0:T(8,128)(2,1)S(1)}, u32[]{:S(2)}, u32[]{:S(2)}) collective-permute-start(bf16[3,64,64]{2,1,0:T(8,128)(2,1)S(1)} %add_convert_fusion), channel_id=1, source_target_pairs={{0,8},{8,16},{16,24},{1,9},{9,17},{17,25},{2,10},{10,18},{18,26},{... | collective-permute-start | bytes 73736 | tf_op jit(solution)/shard_map/ppermute | solution.py:26
  146.4 85.0 %copy-start.15 = (s32[4,2]{0,1:T(2,128)S(1)}, s32[4,2]{0,1:T(2,128)}, u32[]{:S(2)}) copy-start(s32[4,2]{0,1:T(2,128)} %param.37) | copy-start | bytes 100
  146.4 150.4 %all-gather.6.cloned.1.call-start = ((), (), s32[]{:S(2)}) async-start(), calls=%async_computation.3 | async-start | bytes 4128768 | tf_op jit(solution)/shard_map/all_gather | solution.py:211
  148.4 151.4 %copy-start.21 = (f32[3584]{0:T(1024)S(1)}, f32[3584]{0:T(1024)}, u32[]{:S(2)}) copy-start(f32[3584]{0:T(1024)} %param.32) | copy-start | bytes 43012
  230.1 143.0 %all-reduce.2.cloned.1.call-start = ((), (), s32[]{:S(2)}) async-start(), calls=%async_computation.4 | async-start | bytes 393216 | tf_op jit(solution)/shard_map/psum | solution.py:201
  306.6 11.7 %collective-permute-start.4 = (bf16[512,224]{0,1:T(8,128)(2,1)}, bf16[512,224]{0,1:T(8,128)(2,1)S(1)}, u32[]{:S(2)}, u32[]{:S(2)}) collective-permute-start(bf16[512,224]{0,1:T(8,128)(2,1)} %slice.149), channel_id=1, source_target_pairs={{0,8},{8,16},{16,24},{24,0},{1,9},{9,17},{17,25},{25,1},{2,10},{10... | collective-permute-start | bytes 688136 | tf_op jit(solution)/shard_map/ppermute | solution.py:16
  318.2 24.8 %copy-start.10 = (bf16[4,1,512]{2,1,0:T(2,128)(2,1)S(1)}, bf16[4,1,512]{2,1,0:T(2,128)(2,1)}, u32[]{:S(2)}) copy-start(bf16[4,1,512]{2,1,0:T(2,128)(2,1)} %all-gather) | copy-start | bytes 12292
  318.2 24.8 %copy-start.11 = (s32[512]{0:T(512)S(1)}, s32[512]{0:T(512)}, u32[]{:S(2)}) copy-start(s32[512]{0:T(512)} %param.35) | copy-start | bytes 6148
  318.2 24.8 %copy-start.13 = (s32[512]{0:T(512)S(1)}, s32[512]{0:T(512)}, u32[]{:S(2)}) copy-start(s32[512]{0:T(512)} %iota_add_fusion) | copy-start | bytes 6148
  318.3 24.8 %copy-start.16 = (s32[4,1]{0,1:T(1,128)S(1)}, s32[4,1]{0,1:T(1,128)}, u32[]{:S(2)}) copy-start(s32[4,1]{0,1:T(1,128)} %get-tuple-element.228) | copy-start | bytes 52
  318.3 5.6 %collective-permute-start.5 = (bf16[512,224]{0,1:T(8,128)(2,1)S(1)}, bf16[512,224]{0,1:T(8,128)(2,1)}, u32[]{:S(2)}, u32[]{:S(2)}) collective-permute-start(bf16[512,224]{0,1:T(8,128)(2,1)S(1)} %collective-permute-done.4), channel_id=1, source_target_pairs={{0,8},{8,16},{16,24},{24,0},{1,9},{9,17},{17,25},{25,1},{2,10},{10... | collective-permute-start | bytes 688136 | tf_op jit(solution)/shard_map/ppermute | solution.py:16
  320.5 132.0 %reduce-scatter.9.cloned.1.call-start = ((), (), s32[]{:S(2)}) async-start(), calls=%async_computation.6 | async-start | bytes 4128768
  320.5 7.5 %collective-permute-start.6 = (bf16[512,224]{0,1:T(8,128)(2,1)}, bf16[512,224]{0,1:T(8,128)(2,1)S(1)}, u32[]{:S(2)}, u32[]{:S(2)}) collective-permute-start(bf16[512,224]{0,1:T(8,128)(2,1)} %slice.149), channel_id=1, source_target_pairs={{0,24},{8,0},{16,8},{24,16},{1,25},{9,1},{17,9},{25,17},{2,26},{10... | collective-permute-start | bytes 688136 | tf_op jit(solution)/shard_map/ppermute | solution.py:18
  (12 other events, 97.1 us)
Sparse Core Ops, SparseCore 0:
  10.2 69.5 all-gather.3
  146.5 79.2 reduce-scatter.6
  230.2 66.4 all-gather.5
  320.6 30.1 all-reduce.1
  373.2 79.2 reduce-scatter.8
